TPU v7x, 32 devices: a whole 2x2x4 slice. The times are simulated.
32 devices in a mesh: section: 4 (over z), space: 8 (over y, x, core).
Axes of the slice: x: 2, y: 2, z: 4, core: 2. Of those that a mesh axis runs over, the one named last changes fastest.
Arguments:
- act_in: bfloat16 [4, 4096, 512], P('section', 'space'), may hold values from -6 to 6
- stash: bfloat16 [4, 4, 4096, 512], P('section', None, 'space'), may hold values from -6 to 6
- plan: int32 [4], P('section'), may hold values from 0 to 3
- grad_in: bfloat16 [4, 4096, 512], P('section', 'space'), may hold values from -6 to 6
- fwd_owner: int32 [4, 4096], P('section', 'space'), may hold values from 0 to 7, as said below
- stash_owner: int32 [4, 4, 4096], P('section', None, 'space'), may hold values from 0 to 7, as said below
- ln_gain: float32 [4, 512], P('section'), may hold values from 0.5 to 1.5
- qkv_weight: bfloat16 [4, 512, 1536], P('section')
- proj_weight: bfloat16 [4, 512, 512], P('section'), may hold values from -1 to 1
Outputs:
- act_out: bfloat16 [4, 4096, 512], P('section', 'space')
- grad_out: bfloat16 [4, 4096, 512], P('section', 'space')
Inputs may be any that keep to these rules, and one draw needn't show every extreme that they name: `fwd_owner`: within each group of 512 rows of one list, owners never decrease; each group sends 128 rows to a quarter of the owners, 64 rows to half of them and none to the rest; in each list one owner gets 128 rows from every group. `stash_owner`: same law for each section and stored microbatch, independently drawn.
All inputs are finite; a program needn't handle non-finite values.
Results may differ from a plain program's by a relative error of at most 0.004.
The roundings to bfloat16 on the way count: a program that leaves them out, or rounds other values in their place, can miss the bound.
Values may be sent and summed in bfloat16 or wider, within the bound.
A program may use at most 128 MiB of HBM per device.

v0:
```python
import math
import jax
import jax.numpy as jnp
from jax import lax
from jax.sharding import PartitionSpec as P

HEADS = 32
EPS = 1e-05
NEG = -1e30
HEAD_GROUP = 2


def passed_along(value, axis, by):
    size = lax.axis_size(axis)
    pairs = [(i, i + by) for i in range(size) if 0 <= i + by < size]
    return lax.ppermute(value, axis, pairs)


def normalize(rows_in, gain):
    values = rows_in.astype(jnp.float32)
    center = values - jnp.mean(values, axis=-1, keepdims=True)
    spread = jnp.mean(center * center, axis=-1, keepdims=True)
    return center * lax.rsqrt(spread + EPS) * gain


def split_heads(block, head_dim):
    return block.reshape(block.shape[0], block.shape[1] // head_dim, head_dim)


def block_probs(query, key_rows, live, scale):
    score = jnp.einsum("qhd,khd->hqk", query, key_rows, preferred_element_type=jnp.float32) * scale
    score = jnp.where(live[None, None, :], score, NEG)
    top = jnp.max(score, axis=2, keepdims=True)
    expd = jnp.exp(score - top)
    return expd / jnp.sum(expd, axis=2, keepdims=True)


def attend(patch, live, heads):
    width = patch.shape[1] // 3
    head_dim = width // heads
    span = HEAD_GROUP * head_dim
    scale = 1.0 / math.sqrt(head_dim)
    slots = patch.shape[0]

    def one_block(block_index, totals):
        start = block_index * span
        query = split_heads(lax.dynamic_slice_in_dim(patch, start, span, 1), head_dim)
        key_rows = split_heads(lax.dynamic_slice_in_dim(patch, width + start, span, 1), head_dim)
        value_rows = split_heads(
            lax.dynamic_slice_in_dim(patch, 2 * width + start, span, 1), head_dim
        )
        probs = block_probs(query, key_rows, live, scale).astype(jnp.bfloat16)
        result = jnp.einsum(
            "hqk,khd->qhd", probs, value_rows, preferred_element_type=jnp.float32
        ).reshape(slots, span)
        return lax.dynamic_update_slice_in_dim(totals, result, start, 1)

    return lax.fori_loop(0, heads // HEAD_GROUP, one_block, jnp.zeros((slots, width), jnp.float32))


def attend_grad(patch, live, upstream, heads):
    width = patch.shape[1] // 3
    head_dim = width // heads
    span = HEAD_GROUP * head_dim
    scale = 1.0 / math.sqrt(head_dim)
    slots = patch.shape[0]

    def one_block(block_index, totals):
        start = block_index * span
        query = split_heads(lax.dynamic_slice_in_dim(patch, start, span, 1), head_dim)
        key_rows = split_heads(lax.dynamic_slice_in_dim(patch, width + start, span, 1), head_dim)
        value_rows = split_heads(
            lax.dynamic_slice_in_dim(patch, 2 * width + start, span, 1), head_dim
        )
        out_grad = split_heads(lax.dynamic_slice_in_dim(upstream, start, span, 1), head_dim)
        probs = block_probs(query, key_rows, live, scale)
        rounded = probs.astype(jnp.bfloat16)
        prob_grad = jnp.einsum(
            "qhd,khd->hqk", out_grad, value_rows, preferred_element_type=jnp.float32
        )
        value_grad = jnp.einsum(
            "hqk,qhd->khd", rounded, out_grad, preferred_element_type=jnp.float32
        ).reshape(slots, span)
        delta = jnp.sum(prob_grad * probs, axis=2, keepdims=True)
        score_grad = (probs * (prob_grad - delta) * scale).astype(jnp.bfloat16)
        query_grad = jnp.einsum(
            "hqk,khd->qhd", score_grad, key_rows, preferred_element_type=jnp.float32
        ).reshape(slots, span)
        key_grad = jnp.einsum(
            "hqk,qhd->khd", score_grad, query, preferred_element_type=jnp.float32
        ).reshape(slots, span)
        totals = lax.dynamic_update_slice_in_dim(totals, query_grad, start, 1)
        totals = lax.dynamic_update_slice_in_dim(totals, key_grad, width + start, 1)
        return lax.dynamic_update_slice_in_dim(totals, value_grad, 2 * width + start, 1)

    return lax.fori_loop(
        0, heads // HEAD_GROUP, one_block, jnp.zeros((slots, 3 * width), jnp.float32)
    )


def layout(owners, groups, cap):
    rows = owners.shape[0]
    labels = jnp.arange(groups, dtype=jnp.int32)
    onehot = (owners[:, None] == labels[None, :]).astype(jnp.int32)
    counts = jnp.sum(onehot, axis=0)
    offsets = jnp.cumsum(counts) - counts
    slots = jnp.arange(cap, dtype=jnp.int32)
    valid = slots[None, :] < counts[:, None]
    index = jnp.where(valid, offsets[:, None] + slots[None, :], 0)
    rank = jnp.arange(rows, dtype=jnp.int32) - jnp.sum(onehot * offsets[None, :], axis=1)
    back = owners * cap + rank
    return (index, valid, back)


def pack_rows(source, index, valid):
    picked = jnp.take(source, index.reshape(-1), axis=0).reshape(index.shape + (source.shape[1],))
    return jnp.where(valid[..., None], picked, jnp.zeros((), source.dtype))


def project(rows_in, w_qkv):
    return jnp.dot(rows_in, w_qkv, preferred_element_type=jnp.float32).astype(jnp.bfloat16)


def on_device(
    act_in, stash, plan, grad_in, fwd_owner, stash_owner, ln_gain, qkv_weight, proj_weight
):
    groups = lax.axis_size("space")
    rows_in = act_in[0]
    rows = rows_in.shape[0]
    width = rows_in.shape[1]
    cap = 2 * rows // groups
    slots_all = groups * cap
    gain = ln_gain[0]
    w_qkv = qkv_weight[0]
    w_proj = proj_weight[0]
    pick = plan[0]
    stored = lax.dynamic_index_in_dim(stash[0], pick, 0, keepdims=False)
    stored_owners = lax.dynamic_index_in_dim(stash_owner[0], pick, 0, keepdims=False)
    upstream = grad_in[0]
    normed = normalize(rows_in, gain).astype(jnp.bfloat16)
    normed_b = normalize(stored, gain).astype(jnp.bfloat16)
    out_grad = jnp.dot(upstream, w_proj.T, preferred_element_type=jnp.float32).astype(jnp.bfloat16)
    payload = project(normed, w_qkv)
    payload_b = project(normed_b, w_qkv)
    index, valid, back = layout(fwd_owner[0], groups, cap)
    index_b, valid_b, back_b = layout(stored_owners, groups, cap)
    send_rows = pack_rows(payload, index, valid)
    send_flags = valid.astype(jnp.bfloat16)
    send_rows_b = pack_rows(payload_b, index_b, valid_b)
    send_flags_b = valid_b.astype(jnp.bfloat16)
    send_grads = pack_rows(out_grad, index_b, valid_b)
    got_rows, got_flags = (
        lax.all_to_all(send_rows, "space", split_axis=0, concat_axis=0, tiled=True),
        lax.all_to_all(send_flags, "space", split_axis=0, concat_axis=0, tiled=True),
    )
    got_rows_b, got_flags_b = (
        lax.all_to_all(send_rows_b, "space", split_axis=0, concat_axis=0, tiled=True),
        lax.all_to_all(send_flags_b, "space", split_axis=0, concat_axis=0, tiled=True),
    )
    got_grads = lax.all_to_all(send_grads, "space", split_axis=0, concat_axis=0, tiled=True)
    patch = got_rows.reshape(slots_all, got_rows.shape[-1])
    patch_b = got_rows_b.reshape(slots_all, got_rows_b.shape[-1])
    live = got_flags.reshape(slots_all) > 0.5
    live_b = got_flags_b.reshape(slots_all) > 0.5
    attended = attend(patch, live, HEADS).astype(jnp.bfloat16).reshape(groups, cap, width)
    qkv_grads = attend_grad(patch_b, live_b, got_grads.reshape(slots_all, width), HEADS).astype(
        jnp.bfloat16
    )
    slot_qkv = qkv_grads.reshape(groups, cap, 3 * width)
    ret_att = lax.all_to_all(attended, "space", split_axis=0, concat_axis=0, tiled=True)
    ret_grads = lax.all_to_all(slot_qkv, "space", split_axis=0, concat_axis=0, tiled=True)
    grad_rows = jnp.take(ret_grads.reshape(slots_all, 3 * width), back_b, axis=0)
    normed_grad = jnp.dot(grad_rows, w_qkv.T, preferred_element_type=jnp.float32)
    att_rows = jnp.take(ret_att.reshape(slots_all, width), back, axis=0)
    mixed = (
        rows_in.astype(jnp.float32) + jnp.dot(att_rows, w_proj, preferred_element_type=jnp.float32)
    ).astype(jnp.bfloat16)
    unused, pull = jax.vjp(lambda values: normalize(values, gain), stored.astype(jnp.float32))
    input_grad = (upstream.astype(jnp.float32) + pull(normed_grad)[0]).astype(jnp.bfloat16)
    act_out = passed_along(mixed[None], "section", 1)
    grad_out = passed_along(input_grad[None], "section", -1)
    return (act_out, grad_out)


def solution(mesh):
    in_specs = (
        P("section", "space", None),
        P("section", None, "space", None),
        P("section"),
        P("section", "space", None),
        P("section", "space"),
        P("section", None, "space"),
        P("section", None),
        P("section", None, None),
        P("section", None, None),
    )
    out_specs = (P("section", "space", None), P("section", "space", None))
    return jax.shard_map(
        on_device, mesh=mesh, in_specs=in_specs, out_specs=out_specs, check_vma=False
    )
```

profile of v0, /device:TPU:18, one launch (start us, length us, event | category | flops | bytes accessed | tf_op | source)
XLA Modules:
  0.0 1101.2 jit_solution(14951067177431255770)
XLA Ops:
  44.7 9.5 all-to-all-done.5
  72.7 23.9 %all-to-all-done.3 = bf16[8,128,1536]{2,1,0:T(8,128)(2,1)} async-done(((bf16[8,128,1536]{2,1,0:T(8,128)(2,1)}), bf16[8,128,1536]{2,1,0:T(8,128)(2,1)}, u32[]{:S(2)}, u32[]{:S(2)}) %all-to-all-start.3) | async-done | bytes 3145760 | tf_op jit(solution)/shard_map/all_to_all | solution.py:157
  107.6 31.3 %all-to-all-done = bf16[8,128,1536]{2,1,0:T(8,128)(2,1)} async-done(((bf16[8,128,1536]{2,1,0:T(8,128)(2,1)}), bf16[8,128,1536]{2,1,0:T(8,128)(2,1)}, u32[]{:S(2)}, u32[]{:S(2)}) %all-to-all-start) | async-done | bytes 3145760 | tf_op jit(solution)/shard_map/all_to_all | solution.py:153
  143.7 179.0 %while.30 = (s32[]{:T(128)}, bf16[1024,512]{0,1:T(8,128)(2,1)S(1)}, bf16[1024,1536]{0,1:T(8,128)(2,1)}, pred[1024]{0:T(1024)(128)(4,1)S(1)}, s32[]{:T(128)}, /*i...) while((s32[]{:T(128)}, bf16[1024,512]{0,1:T(8,128)(2,1)S(1)}, ...), condition=%wide.region_8.10_spmd, body=%wide.region_5.9_spmd.sunk | while | flops 146801680 | bytes 17581340 | solution.py:58
  144.7 6.2 fusion.130
  155.9 6.2 fusion.130
  167.1 6.2 fusion.130
  178.2 6.2 fusion.130
  189.4 6.2 fusion.130
  200.6 6.2 fusion.130
  211.8 6.2 fusion.130
  223.0 6.2 fusion.130
  245.4 6.2 fusion.130
  256.6 6.2 fusion.130
  267.8 6.2 fusion.130
  278.9 6.2 fusion.130
  290.1 6.2 fusion.130
  301.3 6.2 fusion.130
  312.5 6.2 fusion.130
  331.8 695.5 %while.31 = (s32[]{:T(128)}, bf16[1024,1536]{0,1:T(8,128)(2,1)}, bf16[1024,1536]{0,1:T(8,128)(2,1)}, pred[1024]{0:T(1024)(128)(4,1)S(1)}, bf16[1024,512]{0,1:T(8...) while((s32[]{:T(128)}, bf16[1024,1536]{0,1:T(8,128)(2,1)}, ...), condition=%wide.region_18.20_spmd, body=%wide.region_14.19_spmd.sunk | while | flops 377494528 | bytes 60327216 | solution.py:96
  332.7 6.2 fusion.143
  343.4 12.1 %fusion.145 = bf16[2,16,1024]{2,1,0:T(8,128)(2,1)S(1)} fusion(bf16[1024,2,16]{0,2,1:T(8,128)(2,1)S(1)} %bitcast.217, f32[2,1024,1024]{1,2,0:T(8,128)} %fusion.142, f32[2,1024,1024]{1,2,0:T(8,128)} %get-tuple-element.366, f32[2,1024]{1,0:T(2,128)S(1)} %get-tuple-element.367), kind=kOutput, calls=%fused_computation.35.clone.1 | convolution fusion | flops 81792000 | bytes 16916480 | tf_op jit(solution)/shard_map/while/body/eval_jaxpr/hqk,qhd->khd/dot_general | solution.py:89
  355.5 13.3 %fusion.144 = bf16[2,16,1024]{2,1,0:T(8,128)(2,1)S(1)} fusion(bf16[1024,2,16]{0,2,1:T(8,128)(2,1)S(1)} %bitcast.215, f32[2,1024,1024]{1,2,0:T(8,128)} %fusion.142, f32[2,1024,1024]{1,2,0:T(8,128)} %get-tuple-element.366, f32[2,1024]{1,0:T(2,128)S(1)} %get-tuple-element.367), kind=kOutput, calls=%fused_computation.36.clone.1 | convolution fusion | flops 81792000 | bytes 16916480 | tf_op jit(solution)/shard_map/while/body/eval_jaxpr/hqk,khd->qhd/dot_general | solution.py:86
  376.2 6.2 fusion.143
  386.9 12.1 %fusion.145 = bf16[2,16,1024]{2,1,0:T(8,128)(2,1)S(1)} fusion(bf16[1024,2,16]{0,2,1:T(8,128)(2,1)S(1)} %bitcast.217, f32[2,1024,1024]{1,2,0:T(8,128)} %fusion.142, f32[2,1024,1024]{1,2,0:T(8,128)} %get-tuple-element.366, f32[2,1024]{1,0:T(2,128)S(1)} %get-tuple-element.367), kind=kOutput, calls=%fused_computation.35.clone.1 | convolution fusion | flops 81792000 | bytes 16916480 | tf_op jit(solution)/shard_map/while/body/eval_jaxpr/hqk,qhd->khd/dot_general | solution.py:89
  399.0 13.3 %fusion.144 = bf16[2,16,1024]{2,1,0:T(8,128)(2,1)S(1)} fusion(bf16[1024,2,16]{0,2,1:T(8,128)(2,1)S(1)} %bitcast.215, f32[2,1024,1024]{1,2,0:T(8,128)} %fusion.142, f32[2,1024,1024]{1,2,0:T(8,128)} %get-tuple-element.366, f32[2,1024]{1,0:T(2,128)S(1)} %get-tuple-element.367), kind=kOutput, calls=%fused_computation.36.clone.1 | convolution fusion | flops 81792000 | bytes 16916480 | tf_op jit(solution)/shard_map/while/body/eval_jaxpr/hqk,khd->qhd/dot_general | solution.py:86
  419.7 6.2 fusion.143
  430.3 12.1 %fusion.145 = bf16[2,16,1024]{2,1,0:T(8,128)(2,1)S(1)} fusion(bf16[1024,2,16]{0,2,1:T(8,128)(2,1)S(1)} %bitcast.217, f32[2,1024,1024]{1,2,0:T(8,128)} %fusion.142, f32[2,1024,1024]{1,2,0:T(8,128)} %get-tuple-element.366, f32[2,1024]{1,0:T(2,128)S(1)} %get-tuple-element.367), kind=kOutput, calls=%fused_computation.35.clone.1 | convolution fusion | flops 81792000 | bytes 16916480 | tf_op jit(solution)/shard_map/while/body/eval_jaxpr/hqk,qhd->khd/dot_general | solution.py:89
  442.5 13.3 %fusion.144 = bf16[2,16,1024]{2,1,0:T(8,128)(2,1)S(1)} fusion(bf16[1024,2,16]{0,2,1:T(8,128)(2,1)S(1)} %bitcast.215, f32[2,1024,1024]{1,2,0:T(8,128)} %fusion.142, f32[2,1024,1024]{1,2,0:T(8,128)} %get-tuple-element.366, f32[2,1024]{1,0:T(2,128)S(1)} %get-tuple-element.367), kind=kOutput, calls=%fused_computation.36.clone.1 | convolution fusion | flops 81792000 | bytes 16916480 | tf_op jit(solution)/shard_map/while/body/eval_jaxpr/hqk,khd->qhd/dot_general | solution.py:86
  463.2 6.2 fusion.143
  473.8 12.1 %fusion.145 = bf16[2,16,1024]{2,1,0:T(8,128)(2,1)S(1)} fusion(bf16[1024,2,16]{0,2,1:T(8,128)(2,1)S(1)} %bitcast.217, f32[2,1024,1024]{1,2,0:T(8,128)} %fusion.142, f32[2,1024,1024]{1,2,0:T(8,128)} %get-tuple-element.366, f32[2,1024]{1,0:T(2,128)S(1)} %get-tuple-element.367), kind=kOutput, calls=%fused_computation.35.clone.1 | convolution fusion | flops 81792000 | bytes 16916480 | tf_op jit(solution)/shard_map/while/body/eval_jaxpr/hqk,qhd->khd/dot_general | solution.py:89
  485.9 13.3 %fusion.144 = bf16[2,16,1024]{2,1,0:T(8,128)(2,1)S(1)} fusion(bf16[1024,2,16]{0,2,1:T(8,128)(2,1)S(1)} %bitcast.215, f32[2,1024,1024]{1,2,0:T(8,128)} %fusion.142, f32[2,1024,1024]{1,2,0:T(8,128)} %get-tuple-element.366, f32[2,1024]{1,0:T(2,128)S(1)} %get-tuple-element.367), kind=kOutput, calls=%fused_computation.36.clone.1 | convolution fusion | flops 81792000 | bytes 16916480 | tf_op jit(solution)/shard_map/while/body/eval_jaxpr/hqk,khd->qhd/dot_general | solution.py:86
  517.3 12.1 %fusion.145 = bf16[2,16,1024]{2,1,0:T(8,128)(2,1)S(1)} fusion(bf16[1024,2,16]{0,2,1:T(8,128)(2,1)S(1)} %bitcast.217, f32[2,1024,1024]{1,2,0:T(8,128)} %fusion.142, f32[2,1024,1024]{1,2,0:T(8,128)} %get-tuple-element.366, f32[2,1024]{1,0:T(2,128)S(1)} %get-tuple-element.367), kind=kOutput, calls=%fused_computation.35.clone.1 | convolution fusion | flops 81792000 | bytes 16916480 | tf_op jit(solution)/shard_map/while/body/eval_jaxpr/hqk,qhd->khd/dot_general | solution.py:89
  529.4 13.3 %fusion.144 = bf16[2,16,1024]{2,1,0:T(8,128)(2,1)S(1)} fusion(bf16[1024,2,16]{0,2,1:T(8,128)(2,1)S(1)} %bitcast.215, f32[2,1024,1024]{1,2,0:T(8,128)} %fusion.142, f32[2,1024,1024]{1,2,0:T(8,128)} %get-tuple-element.366, f32[2,1024]{1,0:T(2,128)S(1)} %get-tuple-element.367), kind=kOutput, calls=%fused_computation.36.clone.1 | convolution fusion | flops 81792000 | bytes 16916480 | tf_op jit(solution)/shard_map/while/body/eval_jaxpr/hqk,khd->qhd/dot_general | solution.py:86
  550.1 6.2 fusion.143
  560.8 12.1 %fusion.145 = bf16[2,16,1024]{2,1,0:T(8,128)(2,1)S(1)} fusion(bf16[1024,2,16]{0,2,1:T(8,128)(2,1)S(1)} %bitcast.217, f32[2,1024,1024]{1,2,0:T(8,128)} %fusion.142, f32[2,1024,1024]{1,2,0:T(8,128)} %get-tuple-element.366, f32[2,1024]{1,0:T(2,128)S(1)} %get-tuple-element.367), kind=kOutput, calls=%fused_computation.35.clone.1 | convolution fusion | flops 81792000 | bytes 16916480 | tf_op jit(solution)/shard_map/while/body/eval_jaxpr/hqk,qhd->khd/dot_general | solution.py:89
  572.9 13.3 %fusion.144 = bf16[2,16,1024]{2,1,0:T(8,128)(2,1)S(1)} fusion(bf16[1024,2,16]{0,2,1:T(8,128)(2,1)S(1)} %bitcast.215, f32[2,1024,1024]{1,2,0:T(8,128)} %fusion.142, f32[2,1024,1024]{1,2,0:T(8,128)} %get-tuple-element.366, f32[2,1024]{1,0:T(2,128)S(1)} %get-tuple-element.367), kind=kOutput, calls=%fused_computation.36.clone.1 | convolution fusion | flops 81792000 | bytes 16916480 | tf_op jit(solution)/shard_map/while/body/eval_jaxpr/hqk,khd->qhd/dot_general | solution.py:86
  604.2 12.1 %fusion.145 = bf16[2,16,1024]{2,1,0:T(8,128)(2,1)S(1)} fusion(bf16[1024,2,16]{0,2,1:T(8,128)(2,1)S(1)} %bitcast.217, f32[2,1024,1024]{1,2,0:T(8,128)} %fusion.142, f32[2,1024,1024]{1,2,0:T(8,128)} %get-tuple-element.366, f32[2,1024]{1,0:T(2,128)S(1)} %get-tuple-element.367), kind=kOutput, calls=%fused_computation.35.clone.1 | convolution fusion | flops 81792000 | bytes 16916480 | tf_op jit(solution)/shard_map/while/body/eval_jaxpr/hqk,qhd->khd/dot_general | solution.py:89
  616.3 13.3 %fusion.144 = bf16[2,16,1024]{2,1,0:T(8,128)(2,1)S(1)} fusion(bf16[1024,2,16]{0,2,1:T(8,128)(2,1)S(1)} %bitcast.215, f32[2,1024,1024]{1,2,0:T(8,128)} %fusion.142, f32[2,1024,1024]{1,2,0:T(8,128)} %get-tuple-element.366, f32[2,1024]{1,0:T(2,128)S(1)} %get-tuple-element.367), kind=kOutput, calls=%fused_computation.36.clone.1 | convolution fusion | flops 81792000 | bytes 16916480 | tf_op jit(solution)/shard_map/while/body/eval_jaxpr/hqk,khd->qhd/dot_general | solution.py:86
  637.0 6.2 fusion.143
  647.7 12.1 %fusion.145 = bf16[2,16,1024]{2,1,0:T(8,128)(2,1)S(1)} fusion(bf16[1024,2,16]{0,2,1:T(8,128)(2,1)S(1)} %bitcast.217, f32[2,1024,1024]{1,2,0:T(8,128)} %fusion.142, f32[2,1024,1024]{1,2,0:T(8,128)} %get-tuple-element.366, f32[2,1024]{1,0:T(2,128)S(1)} %get-tuple-element.367), kind=kOutput, calls=%fused_computation.35.clone.1 | convolution fusion | flops 81792000 | bytes 16916480 | tf_op jit(solution)/shard_map/while/body/eval_jaxpr/hqk,qhd->khd/dot_general | solution.py:89
  659.8 13.3 %fusion.144 = bf16[2,16,1024]{2,1,0:T(8,128)(2,1)S(1)} fusion(bf16[1024,2,16]{0,2,1:T(8,128)(2,1)S(1)} %bitcast.215, f32[2,1024,1024]{1,2,0:T(8,128)} %fusion.142, f32[2,1024,1024]{1,2,0:T(8,128)} %get-tuple-element.366, f32[2,1024]{1,0:T(2,128)S(1)} %get-tuple-element.367), kind=kOutput, calls=%fused_computation.36.clone.1 | convolution fusion | flops 81792000 | bytes 16916480 | tf_op jit(solution)/shard_map/while/body/eval_jaxpr/hqk,khd->qhd/dot_general | solution.py:86
  680.5 6.2 fusion.143
  691.2 12.1 %fusion.145 = bf16[2,16,1024]{2,1,0:T(8,128)(2,1)S(1)} fusion(bf16[1024,2,16]{0,2,1:T(8,128)(2,1)S(1)} %bitcast.217, f32[2,1024,1024]{1,2,0:T(8,128)} %fusion.142, f32[2,1024,1024]{1,2,0:T(8,128)} %get-tuple-element.366, f32[2,1024]{1,0:T(2,128)S(1)} %get-tuple-element.367), kind=kOutput, calls=%fused_computation.35.clone.1 | convolution fusion | flops 81792000 | bytes 16916480 | tf_op jit(solution)/shard_map/while/body/eval_jaxpr/hqk,qhd->khd/dot_general | solution.py:89
  703.3 13.3 %fusion.144 = bf16[2,16,1024]{2,1,0:T(8,128)(2,1)S(1)} fusion(bf16[1024,2,16]{0,2,1:T(8,128)(2,1)S(1)} %bitcast.215, f32[2,1024,1024]{1,2,0:T(8,128)} %fusion.142, f32[2,1024,1024]{1,2,0:T(8,128)} %get-tuple-element.366, f32[2,1024]{1,0:T(2,128)S(1)} %get-tuple-element.367), kind=kOutput, calls=%fused_computation.36.clone.1 | convolution fusion | flops 81792000 | bytes 16916480 | tf_op jit(solution)/shard_map/while/body/eval_jaxpr/hqk,khd->qhd/dot_general | solution.py:86
  724.0 6.2 fusion.143
  734.6 12.1 %fusion.145 = bf16[2,16,1024]{2,1,0:T(8,128)(2,1)S(1)} fusion(bf16[1024,2,16]{0,2,1:T(8,128)(2,1)S(1)} %bitcast.217, f32[2,1024,1024]{1,2,0:T(8,128)} %fusion.142, f32[2,1024,1024]{1,2,0:T(8,128)} %get-tuple-element.366, f32[2,1024]{1,0:T(2,128)S(1)} %get-tuple-element.367), kind=kOutput, calls=%fused_computation.35.clone.1 | convolution fusion | flops 81792000 | bytes 16916480 | tf_op jit(solution)/shard_map/while/body/eval_jaxpr/hqk,qhd->khd/dot_general | solution.py:89
  746.7 13.3 %fusion.144 = bf16[2,16,1024]{2,1,0:T(8,128)(2,1)S(1)} fusion(bf16[1024,2,16]{0,2,1:T(8,128)(2,1)S(1)} %bitcast.215, f32[2,1024,1024]{1,2,0:T(8,128)} %fusion.142, f32[2,1024,1024]{1,2,0:T(8,128)} %get-tuple-element.366, f32[2,1024]{1,0:T(2,128)S(1)} %get-tuple-element.367), kind=kOutput, calls=%fused_computation.36.clone.1 | convolution fusion | flops 81792000 | bytes 16916480 | tf_op jit(solution)/shard_map/while/body/eval_jaxpr/hqk,khd->qhd/dot_general | solution.py:86
  778.1 12.1 %fusion.145 = bf16[2,16,1024]{2,1,0:T(8,128)(2,1)S(1)} fusion(bf16[1024,2,16]{0,2,1:T(8,128)(2,1)S(1)} %bitcast.217, f32[2,1024,1024]{1,2,0:T(8,128)} %fusion.142, f32[2,1024,1024]{1,2,0:T(8,128)} %get-tuple-element.366, f32[2,1024]{1,0:T(2,128)S(1)} %get-tuple-element.367), kind=kOutput, calls=%fused_computation.35.clone.1 | convolution fusion | flops 81792000 | bytes 16916480 | tf_op jit(solution)/shard_map/while/body/eval_jaxpr/hqk,qhd->khd/dot_general | solution.py:89
  790.2 13.3 %fusion.144 = bf16[2,16,1024]{2,1,0:T(8,128)(2,1)S(1)} fusion(bf16[1024,2,16]{0,2,1:T(8,128)(2,1)S(1)} %bitcast.215, f32[2,1024,1024]{1,2,0:T(8,128)} %fusion.142, f32[2,1024,1024]{1,2,0:T(8,128)} %get-tuple-element.366, f32[2,1024]{1,0:T(2,128)S(1)} %get-tuple-element.367), kind=kOutput, calls=%fused_computation.36.clone.1 | convolution fusion | flops 81792000 | bytes 16916480 | tf_op jit(solution)/shard_map/while/body/eval_jaxpr/hqk,khd->qhd/dot_general | solution.py:86
  810.9 6.2 fusion.143
  821.6 12.1 %fusion.145 = bf16[2,16,1024]{2,1,0:T(8,128)(2,1)S(1)} fusion(bf16[1024,2,16]{0,2,1:T(8,128)(2,1)S(1)} %bitcast.217, f32[2,1024,1024]{1,2,0:T(8,128)} %fusion.142, f32[2,1024,1024]{1,2,0:T(8,128)} %get-tuple-element.366, f32[2,1024]{1,0:T(2,128)S(1)} %get-tuple-element.367), kind=kOutput, calls=%fused_computation.35.clone.1 | convolution fusion | flops 81792000 | bytes 16916480 | tf_op jit(solution)/shard_map/while/body/eval_jaxpr/hqk,qhd->khd/dot_general | solution.py:89
  833.7 13.3 %fusion.144 = bf16[2,16,1024]{2,1,0:T(8,128)(2,1)S(1)} fusion(bf16[1024,2,16]{0,2,1:T(8,128)(2,1)S(1)} %bitcast.215, f32[2,1024,1024]{1,2,0:T(8,128)} %fusion.142, f32[2,1024,1024]{1,2,0:T(8,128)} %get-tuple-element.366, f32[2,1024]{1,0:T(2,128)S(1)} %get-tuple-element.367), kind=kOutput, calls=%fused_computation.36.clone.1 | convolution fusion | flops 81792000 | bytes 16916480 | tf_op jit(solution)/shard_map/while/body/eval_jaxpr/hqk,khd->qhd/dot_general | solution.py:86
  865.0 12.1 %fusion.145 = bf16[2,16,1024]{2,1,0:T(8,128)(2,1)S(1)} fusion(bf16[1024,2,16]{0,2,1:T(8,128)(2,1)S(1)} %bitcast.217, f32[2,1024,1024]{1,2,0:T(8,128)} %fusion.142, f32[2,1024,1024]{1,2,0:T(8,128)} %get-tuple-element.366, f32[2,1024]{1,0:T(2,128)S(1)} %get-tuple-element.367), kind=kOutput, calls=%fused_computation.35.clone.1 | convolution fusion | flops 81792000 | bytes 16916480 | tf_op jit(solution)/shard_map/while/body/eval_jaxpr/hqk,qhd->khd/dot_general | solution.py:89
  877.1 13.3 %fusion.144 = bf16[2,16,1024]{2,1,0:T(8,128)(2,1)S(1)} fusion(bf16[1024,2,16]{0,2,1:T(8,128)(2,1)S(1)} %bitcast.215, f32[2,1024,1024]{1,2,0:T(8,128)} %fusion.142, f32[2,1024,1024]{1,2,0:T(8,128)} %get-tuple-element.366, f32[2,1024]{1,0:T(2,128)S(1)} %get-tuple-element.367), kind=kOutput, calls=%fused_computation.36.clone.1 | convolution fusion | flops 81792000 | bytes 16916480 | tf_op jit(solution)/shard_map/while/body/eval_jaxpr/hqk,khd->qhd/dot_general | solution.py:86
  908.5 12.1 %fusion.145 = bf16[2,16,1024]{2,1,0:T(8,128)(2,1)S(1)} fusion(bf16[1024,2,16]{0,2,1:T(8,128)(2,1)S(1)} %bitcast.217, f32[2,1024,1024]{1,2,0:T(8,128)} %fusion.142, f32[2,1024,1024]{1,2,0:T(8,128)} %get-tuple-element.366, f32[2,1024]{1,0:T(2,128)S(1)} %get-tuple-element.367), kind=kOutput, calls=%fused_computation.35.clone.1 | convolution fusion | flops 81792000 | bytes 16916480 | tf_op jit(solution)/shard_map/while/body/eval_jaxpr/hqk,qhd->khd/dot_general | solution.py:89
  920.6 13.3 %fusion.144 = bf16[2,16,1024]{2,1,0:T(8,128)(2,1)S(1)} fusion(bf16[1024,2,16]{0,2,1:T(8,128)(2,1)S(1)} %bitcast.215, f32[2,1024,1024]{1,2,0:T(8,128)} %fusion.142, f32[2,1024,1024]{1,2,0:T(8,128)} %get-tuple-element.366, f32[2,1024]{1,0:T(2,128)S(1)} %get-tuple-element.367), kind=kOutput, calls=%fused_computation.36.clone.1 | convolution fusion | flops 81792000 | bytes 16916480 | tf_op jit(solution)/shard_map/while/body/eval_jaxpr/hqk,khd->qhd/dot_general | solution.py:86
  952.0 12.1 %fusion.145 = bf16[2,16,1024]{2,1,0:T(8,128)(2,1)S(1)} fusion(bf16[1024,2,16]{0,2,1:T(8,128)(2,1)S(1)} %bitcast.217, f32[2,1024,1024]{1,2,0:T(8,128)} %fusion.142, f32[2,1024,1024]{1,2,0:T(8,128)} %get-tuple-element.366, f32[2,1024]{1,0:T(2,128)S(1)} %get-tuple-element.367), kind=kOutput, calls=%fused_computation.35.clone.1 | convolution fusion | flops 81792000 | bytes 16916480 | tf_op jit(solution)/shard_map/while/body/eval_jaxpr/hqk,qhd->khd/dot_general | solution.py:89
  964.1 13.3 %fusion.144 = bf16[2,16,1024]{2,1,0:T(8,128)(2,1)S(1)} fusion(bf16[1024,2,16]{0,2,1:T(8,128)(2,1)S(1)} %bitcast.215, f32[2,1024,1024]{1,2,0:T(8,128)} %fusion.142, f32[2,1024,1024]{1,2,0:T(8,128)} %get-tuple-element.366, f32[2,1024]{1,0:T(2,128)S(1)} %get-tuple-element.367), kind=kOutput, calls=%fused_computation.36.clone.1 | convolution fusion | flops 81792000 | bytes 16916480 | tf_op jit(solution)/shard_map/while/body/eval_jaxpr/hqk,khd->qhd/dot_general | solution.py:86
  984.8 6.2 fusion.143
  995.4 12.1 %fusion.145 = bf16[2,16,1024]{2,1,0:T(8,128)(2,1)S(1)} fusion(bf16[1024,2,16]{0,2,1:T(8,128)(2,1)S(1)} %bitcast.217, f32[2,1024,1024]{1,2,0:T(8,128)} %fusion.142, f32[2,1024,1024]{1,2,0:T(8,128)} %get-tuple-element.366, f32[2,1024]{1,0:T(2,128)S(1)} %get-tuple-element.367), kind=kOutput, calls=%fused_computation.35.clone.1 | convolution fusion | flops 81792000 | bytes 16916480 | tf_op jit(solution)/shard_map/while/body/eval_jaxpr/hqk,qhd->khd/dot_general | solution.py:89
  1007.5 13.3 %fusion.144 = bf16[2,16,1024]{2,1,0:T(8,128)(2,1)S(1)} fusion(bf16[1024,2,16]{0,2,1:T(8,128)(2,1)S(1)} %bitcast.215, f32[2,1024,1024]{1,2,0:T(8,128)} %fusion.142, f32[2,1024,1024]{1,2,0:T(8,128)} %get-tuple-element.366, f32[2,1024]{1,0:T(2,128)S(1)} %get-tuple-element.367), kind=kOutput, calls=%fused_computation.36.clone.1 | convolution fusion | flops 81792000 | bytes 16916480 | tf_op jit(solution)/shard_map/while/body/eval_jaxpr/hqk,khd->qhd/dot_general | solution.py:86
  1046.4 26.9 %all-to-all-done.6 = bf16[8,128,1536]{2,1,0:T(8,128)(2,1)} async-done(((bf16[8,128,1536]{2,1,0:T(8,128)(2,1)}), bf16[8,128,1536]{2,1,0:T(8,128)(2,1)}, u32[]{:S(2)}, u32[]{:S(2)}) %all-to-all-start.6) | async-done | bytes 3145760 | tf_op jit(solution)/shard_map/all_to_all | solution.py:171
  1084.9 13.4 %collective-permute-done.1 = bf16[1,512,512]{1,2,0:T(8,128)(2,1)S(1)} collective-permute-done((bf16[1,512,512]{1,2,0:T(8,128)(2,1)S(1)}, bf16[1,512,512]{1,2,0:T(8,128)(2,1)S(1)}, u32[]{:S(2)}, u32[]{:S(2)}) %collective-permute-start.1) | collective-permute-done | bytes 524320 | tf_op jit(solution)/shard_map/ppermute | solution.py:16
  (283 shorter events, 432.7 us)
Async XLA Ops:
  0.6 7.7 copy-start
  0.6 8.3 copy-start.12
  0.7 8.8 copy-start.24
  2.2 0.6 copy-start.14
  3.6 24.5 %all-to-all-start.4 = ((bf16[8,1,128]{2,1,0:T(2,128)(2,1)}), bf16[8,1,128]{2,1,0:T(2,128)(2,1)S(1)}, u32[]{:S(2)}, u32[]{:S(2)}) async-start(bf16[8,1,128]{2,1,0:T(2,128)(2,1)} %compare_convert_fusion), calls=%async_computation.4 | async-start | bytes 8192 | tf_op jit(solution)/shard_map/all_to_all | solution.py:158
  8.0 0.9 copy-start.20
  8.6 3.4 copy-start.2
  8.7 0.8 copy-start.10
  8.9 0.6 copy-start.18
  8.9 0.6 copy-start.16
  17.6 4.0 copy-start.4
  17.6 4.0 copy-start.8
  22.1 10.1 copy-start.6
  28.0 7.3 all-to-all-start.1
  35.4 18.8 %all-to-all-start.5 = ((bf16[8,128,512]{2,1,0:T(8,128)(2,1)}), bf16[8,128,512]{2,1,0:T(8,128)(2,1)S(1)}, u32[]{:S(2)}, u32[]{:S(2)}) async-start(bf16[8,128,512]{2,1,0:T(8,128)(2,1)} %select_select_fusion), calls=%async_computation.5 | async-start | bytes 2097152 | tf_op jit(solution)/shard_map/all_to_all | solution.py:160
  54.2 42.3 %all-to-all-start.3 = ((bf16[8,128,1536]{2,1,0:T(8,128)(2,1)}), bf16[8,128,1536]{2,1,0:T(8,128)(2,1)}, u32[]{:S(2)}, u32[]{:S(2)}) async-start(bf16[8,128,1536]{2,1,0:T(8,128)(2,1)} %broadcast_select_fusion.2), calls=%async_computation.3 | async-start | bytes 6291456 | tf_op jit(solution)/shard_map/all_to_all | solution.py:157
  60.1 8.3 copy-start.22
  96.5 42.3 %all-to-all-start = ((bf16[8,128,1536]{2,1,0:T(8,128)(2,1)}), bf16[8,128,1536]{2,1,0:T(8,128)(2,1)}, u32[]{:S(2)}, u32[]{:S(2)}) async-start(bf16[8,128,1536]{2,1,0:T(8,128)(2,1)} %broadcast_select_fusion.3), calls=%async_computation | async-start | bytes 6291456 | tf_op jit(solution)/shard_map/all_to_all | solution.py:153
  324.1 707.9 %all-to-all-start.2 = ((bf16[8,128,512]{2,1,0:T(8,128)(2,1)}), bf16[8,128,512]{2,1,0:T(8,128)(2,1)}, u32[]{:S(2)}, u32[]{:S(2)}) async-start(bf16[8,128,512]{2,1,0:T(8,128)(2,1)} %bitcast.26), calls=%async_computation.2 | async-start | bytes 2097152 | tf_op jit(solution)/shard_map/all_to_all | solution.py:170
  1032.0 4.8 copy-start.5
  1032.0 5.0 copy-start.15
  1032.0 5.1 copy-start.21
  1032.0 5.9 copy-start.13
  1032.0 5.9 copy-start.23
  1032.0 41.3 %all-to-all-start.6 = ((bf16[8,128,1536]{2,1,0:T(8,128)(2,1)}), bf16[8,128,1536]{2,1,0:T(8,128)(2,1)}, u32[]{:S(2)}, u32[]{:S(2)}) async-start(bf16[8,128,1536]{2,1,0:T(8,128)(2,1)} %bitcast.199), calls=%async_computation.6 | async-start | bytes 6291456 | tf_op jit(solution)/shard_map/all_to_all | solution.py:171
  1036.8 4.6 copy-start.7
  1036.8 4.6 copy-start.9
  1042.7 42.2 %collective-permute-start = (bf16[1,512,512]{2,1,0:T(8,128)(2,1)}, bf16[1,512,512]{2,1,0:T(8,128)(2,1)}, u32[]{:S(2)}, u32[]{:S(2)}) collective-permute-start(bf16[1,512,512]{2,1,0:T(8,128)(2,1)} %fusion.48), channel_id=1, source_target_pairs={{0,8},{8,16},{16,24},{1,9},{9,17},{17,25},{2,10},{10,18},{18,26},{... | collective-permute-start | bytes 1572872 | tf_op jit(solution)/shard_map/ppermute | solution.py:16
  1073.3 6.0 copy-start.3
  1073.3 6.0 copy-start.11
  1073.3 6.0 copy-start.25
  1079.3 2.5 copy-start.19
  1079.3 2.6 copy-start.17
  1081.8 19.3 %copy-start.1 = (bf16[1,4,512,512]{3,2,1,0:T(8,128)(2,1)S(1)}, bf16[1,4,512,512]{3,2,1,0:T(8,128)(2,1)}, u32[]{:S(2)}) copy-start(bf16[1,4,512,512]{3,2,1,0:T(8,128)(2,1)} %param.16) | copy-start | bytes 6291460
  1082.5 15.8 %collective-permute-start.1 = (bf16[1,512,512]{1,2,0:T(8,128)(2,1)S(1)}, bf16[1,512,512]{1,2,0:T(8,128)(2,1)S(1)}, u32[]{:S(2)}, u32[]{:S(2)}) collective-permute-start(bf16[1,512,512]{1,2,0:T(8,128)(2,1)S(1)} %fusion.64), channel_id=1, source_target_pairs={{8,0},{16,8},{24,16},{9,1},{17,9},{25,17},{10,2},{18,10},{26,18},{... | collective-permute-start | bytes 1572872 | tf_op jit(solution)/shard_map/ppermute | solution.py:16
where the time goes:
time: 1110 us; the launch traced here: 1100 us
  matrix products  823 us (74%)
  local copies, waits for them, and re-layouts  108 us (10%)
  waiting for transfers between devices  108 us (10%)
  starting transfers between devices  41.5 us (4%)
  other arithmetic  18.2 us (2%)
    dot_general x16, matrix products, one_block(): jnp.einsum('hqk,khd->qhd', score_grad, key_rows, preferred_element_type=j...  213 us
    sub x32, matrix products, block_probs(): expd = jnp.exp(score - top)  197 us
    dot_general x16, matrix products, one_block(): jnp.einsum('hqk,qhd->khd', score_grad, query, preferred_element_type=jnp....  194 us
    dot_general x16, matrix products, one_block(): jnp.einsum('hqk,qhd->khd', rounded, out_grad, preferred_element_type=jnp....  73.1 us
    dot_general x16, matrix products, one_block(): jnp.einsum('qhd,khd->hqk', out_grad, value_rows, preferred_element_type=j...  72 us
    dot_general x16, matrix products, one_block(): jnp.einsum('hqk,khd->qhd', probs, value_rows, preferred_element_type=jnp....  64.8 us
    all_to_all x1, waiting for transfers between devices, on_device(): lax.all_to_all(send_rows, 'space', split_axis=0, concat_axis=0, tiled=True)  31.3 us
    all_to_all x1, waiting for transfers between devices, on_device(): lax.all_to_all(slot_qkv, 'space', split_axis=0, concat_axis=0, tiled=True)  26.9 us
  transfers between devices with their start and end apart: 9, of which 6 were waited for; matrix products, arithmetic and copies ran while one was open for 69% of the time, Pallas kernels for 0%

commit v1 on v0

--- a/solution.py
+++ b/solution.py
@@ -3,6 +3,7 @@
 import jax.numpy as jnp
 from jax import lax
 from jax.sharding import PartitionSpec as P
+from jax.lax import axis_index, axis_size, ppermute
 
 HEADS = 32
 EPS = 1e-05
@@ -168,7 +169,22 @@
     )
     slot_qkv = qkv_grads.reshape(groups, cap, 3 * width)
     ret_att = lax.all_to_all(attended, "space", split_axis=0, concat_axis=0, tiled=True)
-    ret_grads = lax.all_to_all(slot_qkv, "space", split_axis=0, concat_axis=0, tiled=True)
+    tall = axis_size("space")
+    v_next = axis_index("space")
+    right_arr, all_rows = (tall, v_next)
+    carry = slot_qkv.shape[0] // right_arr
+    current_value = list(slot_qkv.shape)
+    current_value[0] = carry
+    main = current_value[0]
+    current_value[0] = main * right_arr
+    ret_grads = jnp.zeros(current_value, slot_qkv.dtype)
+    for dev_i in range(right_arr):
+        odd = lax.dynamic_slice_in_dim(slot_qkv, (all_rows ^ dev_i) * carry, carry, axis=0)
+        if dev_i:
+            odd = ppermute(odd, "space", [(d, d ^ dev_i) for d in range(right_arr)])
+        ret_grads = lax.dynamic_update_slice_in_dim(
+            ret_grads, odd, (all_rows ^ dev_i) * main, axis=0
+        )
     grad_rows = jnp.take(ret_grads.reshape(slots_all, 3 * width), back_b, axis=0)
     normed_grad = jnp.dot(grad_rows, w_qkv.T, preferred_element_type=jnp.float32)
     att_rows = jnp.take(ret_att.reshape(slots_all, width), back, axis=0)

time: 1110 us -> 1060 us (0.955)
  waiting for transfers between devices: 108 us -> 64.8 us
  local copies, waits for them, and re-layouts: 108 us -> 95.3 us
    all_to_all x1, waiting for transfers between devices: 31.3 us -> 0.01 us  [on_device(): lax.all_to_all(send_rows, 'space', split_axis=0, concat_axis=0, tiled=True)]
    all_to_all x1 -> x0, waiting for transfers between devices: 26.9 us -> none  [on_device(): lax.all_to_all(slot_qkv, 'space', split_axis=0, concat_axis=0, tiled=True)]
    ppermute x0 -> x7, waiting for transfers between devices: none -> 22.6 us  [on_device(): odd = ppermute(odd, 'space', [(d, d ^ dev_i) for d in range(right_arr)])]
  transfers between devices with their start and end apart: 9 -> 15, of which waited for: 6 -> 7; matrix products, arithmetic and copies ran while one was open for 69% -> 89% of each run, Pallas kernels for 0% -> 0%
where the time goes in v1:
time: 1060 us; the launch traced here: 1050 us
  matrix products  824 us (78%)
  local copies, waits for them, and re-layouts  95.3 us (9%)
  waiting for transfers between devices  64.8 us (6%)
  starting transfers between devices  41.5 us (4%)
  other arithmetic  21.6 us (2%)
    dot_general x16, matrix products, one_block(): jnp.einsum('hqk,khd->qhd', score_grad, key_rows, preferred_element_type=j...  213 us
    sub x32, matrix products, block_probs(): expd = jnp.exp(score - top)  197 us
    dot_general x16, matrix products, one_block(): jnp.einsum('hqk,qhd->khd', score_grad, query, preferred_element_type=jnp....  194 us
    dot_general x16, matrix products, one_block(): jnp.einsum('hqk,qhd->khd', rounded, out_grad, preferred_element_type=jnp....  73.1 us
    dot_general x16, matrix products, one_block(): jnp.einsum('qhd,khd->hqk', out_grad, value_rows, preferred_element_type=j...  72.1 us
    dot_general x16, matrix products, one_block(): jnp.einsum('hqk,khd->qhd', probs, value_rows, preferred_element_type=jnp....  64.8 us
    all_to_all x1, waiting for transfers between devices, on_device(): lax.all_to_all(send_rows_b, 'space', split_axis=0, concat_axis=0, tiled=T...  27.6 us
    ppermute x7, waiting for transfers between devices, on_device(): odd = ppermute(odd, 'space', [(d, d ^ dev_i) for d in range(right_arr)])  22.6 us
  transfers between devices with their start and end apart: 15, of which 7 were waited for; matrix products, arithmetic and copies ran while one was open for 89% of the time, Pallas kernels for 0%

profile of v1, /device:TPU:18, one launch (start us, length us, event | category | flops | bytes accessed | tf_op | source)
XLA Modules:
  0.0 1050.2 jit_solution(11249410290221488112)
XLA Ops:
  70.9 27.6 %all-to-all-done.3 = bf16[8,128,1536]{2,1,0:T(8,128)(2,1)S(1)} async-done(((bf16[8,128,1536]{2,1,0:T(8,128)(2,1)}), bf16[8,128,1536]{2,1,0:T(8,128)(2,1)S(1)}, u32[]{:S(2)}, u32[]{:S(2)}) %all-to-all-start.3) | async-done | bytes 3145760 | tf_op jit(solution)/shard_map/all_to_all | solution.py:158
  107.6 667.9 %while.31 = (s32[]{:T(128)}, bf16[1024,1536]{0,1:T(8,128)(2,1)S(1)}, bf16[1024,1536]{0,1:T(8,128)(2,1)}, pred[1024]{0:T(1024)(128)(4,1)S(1)}, bf16[1024,512]{0,1...) while((s32[]{:T(128)}, ...), condition=%wide.region_18.20_spmd, body=%wide.region_14.19_spmd.sunk | while | flops 377494528 | bytes 60327216 | solution.py:97
  108.6 6.2 fusion.143
  119.3 12.1 %fusion.145 = bf16[2,16,1024]{2,1,0:T(8,128)(2,1)S(1)} fusion(bf16[1024,2,16]{0,2,1:T(8,128)(2,1)S(1)} %bitcast.220, f32[2,1024,1024]{1,2,0:T(8,128)} %fusion.142, f32[2,1024,1024]{1,2,0:T(8,128)} %get-tuple-element.374, f32[2,1024]{1,0:T(2,128)S(1)} %get-tuple-element.375), kind=kOutput, calls=%fused_computation.35.clone.1 | convolution fusion | flops 81792000 | bytes 16916480 | tf_op jit(solution)/shard_map/while/body/eval_jaxpr/hqk,qhd->khd/dot_general | solution.py:90
  131.4 13.3 %fusion.144 = bf16[2,16,1024]{2,1,0:T(8,128)(2,1)S(1)} fusion(bf16[1024,2,16]{0,2,1:T(8,128)(2,1)S(1)} %bitcast.218, f32[2,1024,1024]{1,2,0:T(8,128)} %fusion.142, f32[2,1024,1024]{1,2,0:T(8,128)} %get-tuple-element.374, f32[2,1024]{1,0:T(2,128)S(1)} %get-tuple-element.375), kind=kOutput, calls=%fused_computation.36.clone.1 | convolution fusion | flops 81792000 | bytes 16916480 | tf_op jit(solution)/shard_map/while/body/eval_jaxpr/hqk,khd->qhd/dot_general | solution.py:87
  150.4 6.2 fusion.143
  161.1 12.1 %fusion.145 = bf16[2,16,1024]{2,1,0:T(8,128)(2,1)S(1)} fusion(bf16[1024,2,16]{0,2,1:T(8,128)(2,1)S(1)} %bitcast.220, f32[2,1024,1024]{1,2,0:T(8,128)} %fusion.142, f32[2,1024,1024]{1,2,0:T(8,128)} %get-tuple-element.374, f32[2,1024]{1,0:T(2,128)S(1)} %get-tuple-element.375), kind=kOutput, calls=%fused_computation.35.clone.1 | convolution fusion | flops 81792000 | bytes 16916480 | tf_op jit(solution)/shard_map/while/body/eval_jaxpr/hqk,qhd->khd/dot_general | solution.py:90
  173.2 13.3 %fusion.144 = bf16[2,16,1024]{2,1,0:T(8,128)(2,1)S(1)} fusion(bf16[1024,2,16]{0,2,1:T(8,128)(2,1)S(1)} %bitcast.218, f32[2,1024,1024]{1,2,0:T(8,128)} %fusion.142, f32[2,1024,1024]{1,2,0:T(8,128)} %get-tuple-element.374, f32[2,1024]{1,0:T(2,128)S(1)} %get-tuple-element.375), kind=kOutput, calls=%fused_computation.36.clone.1 | convolution fusion | flops 81792000 | bytes 16916480 | tf_op jit(solution)/shard_map/while/body/eval_jaxpr/hqk,khd->qhd/dot_general | solution.py:87
  192.1 6.2 fusion.143
  202.8 12.1 %fusion.145 = bf16[2,16,1024]{2,1,0:T(8,128)(2,1)S(1)} fusion(bf16[1024,2,16]{0,2,1:T(8,128)(2,1)S(1)} %bitcast.220, f32[2,1024,1024]{1,2,0:T(8,128)} %fusion.142, f32[2,1024,1024]{1,2,0:T(8,128)} %get-tuple-element.374, f32[2,1024]{1,0:T(2,128)S(1)} %get-tuple-element.375), kind=kOutput, calls=%fused_computation.35.clone.1 | convolution fusion | flops 81792000 | bytes 16916480 | tf_op jit(solution)/shard_map/while/body/eval_jaxpr/hqk,qhd->khd/dot_general | solution.py:90
  214.9 13.3 %fusion.144 = bf16[2,16,1024]{2,1,0:T(8,128)(2,1)S(1)} fusion(bf16[1024,2,16]{0,2,1:T(8,128)(2,1)S(1)} %bitcast.218, f32[2,1024,1024]{1,2,0:T(8,128)} %fusion.142, f32[2,1024,1024]{1,2,0:T(8,128)} %get-tuple-element.374, f32[2,1024]{1,0:T(2,128)S(1)} %get-tuple-element.375), kind=kOutput, calls=%fused_computation.36.clone.1 | convolution fusion | flops 81792000 | bytes 16916480 | tf_op jit(solution)/shard_map/while/body/eval_jaxpr/hqk,khd->qhd/dot_general | solution.py:87
  233.9 6.2 fusion.143
  244.5 12.1 %fusion.145 = bf16[2,16,1024]{2,1,0:T(8,128)(2,1)S(1)} fusion(bf16[1024,2,16]{0,2,1:T(8,128)(2,1)S(1)} %bitcast.220, f32[2,1024,1024]{1,2,0:T(8,128)} %fusion.142, f32[2,1024,1024]{1,2,0:T(8,128)} %get-tuple-element.374, f32[2,1024]{1,0:T(2,128)S(1)} %get-tuple-element.375), kind=kOutput, calls=%fused_computation.35.clone.1 | convolution fusion | flops 81792000 | bytes 16916480 | tf_op jit(solution)/shard_map/while/body/eval_jaxpr/hqk,qhd->khd/dot_general | solution.py:90
  256.6 13.3 %fusion.144 = bf16[2,16,1024]{2,1,0:T(8,128)(2,1)S(1)} fusion(bf16[1024,2,16]{0,2,1:T(8,128)(2,1)S(1)} %bitcast.218, f32[2,1024,1024]{1,2,0:T(8,128)} %fusion.142, f32[2,1024,1024]{1,2,0:T(8,128)} %get-tuple-element.374, f32[2,1024]{1,0:T(2,128)S(1)} %get-tuple-element.375), kind=kOutput, calls=%fused_computation.36.clone.1 | convolution fusion | flops 81792000 | bytes 16916480 | tf_op jit(solution)/shard_map/while/body/eval_jaxpr/hqk,khd->qhd/dot_general | solution.py:87
  275.6 6.2 fusion.143
  286.3 12.1 %fusion.145 = bf16[2,16,1024]{2,1,0:T(8,128)(2,1)S(1)} fusion(bf16[1024,2,16]{0,2,1:T(8,128)(2,1)S(1)} %bitcast.220, f32[2,1024,1024]{1,2,0:T(8,128)} %fusion.142, f32[2,1024,1024]{1,2,0:T(8,128)} %get-tuple-element.374, f32[2,1024]{1,0:T(2,128)S(1)} %get-tuple-element.375), kind=kOutput, calls=%fused_computation.35.clone.1 | convolution fusion | flops 81792000 | bytes 16916480 | tf_op jit(solution)/shard_map/while/body/eval_jaxpr/hqk,qhd->khd/dot_general | solution.py:90
  298.4 13.3 %fusion.144 = bf16[2,16,1024]{2,1,0:T(8,128)(2,1)S(1)} fusion(bf16[1024,2,16]{0,2,1:T(8,128)(2,1)S(1)} %bitcast.218, f32[2,1024,1024]{1,2,0:T(8,128)} %fusion.142, f32[2,1024,1024]{1,2,0:T(8,128)} %get-tuple-element.374, f32[2,1024]{1,0:T(2,128)S(1)} %get-tuple-element.375), kind=kOutput, calls=%fused_computation.36.clone.1 | convolution fusion | flops 81792000 | bytes 16916480 | tf_op jit(solution)/shard_map/while/body/eval_jaxpr/hqk,khd->qhd/dot_general | solution.py:87
  317.4 6.2 fusion.143
  328.0 12.1 %fusion.145 = bf16[2,16,1024]{2,1,0:T(8,128)(2,1)S(1)} fusion(bf16[1024,2,16]{0,2,1:T(8,128)(2,1)S(1)} %bitcast.220, f32[2,1024,1024]{1,2,0:T(8,128)} %fusion.142, f32[2,1024,1024]{1,2,0:T(8,128)} %get-tuple-element.374, f32[2,1024]{1,0:T(2,128)S(1)} %get-tuple-element.375), kind=kOutput, calls=%fused_computation.35.clone.1 | convolution fusion | flops 81792000 | bytes 16916480 | tf_op jit(solution)/shard_map/while/body/eval_jaxpr/hqk,qhd->khd/dot_general | solution.py:90
  340.1 13.3 %fusion.144 = bf16[2,16,1024]{2,1,0:T(8,128)(2,1)S(1)} fusion(bf16[1024,2,16]{0,2,1:T(8,128)(2,1)S(1)} %bitcast.218, f32[2,1024,1024]{1,2,0:T(8,128)} %fusion.142, f32[2,1024,1024]{1,2,0:T(8,128)} %get-tuple-element.374, f32[2,1024]{1,0:T(2,128)S(1)} %get-tuple-element.375), kind=kOutput, calls=%fused_computation.36.clone.1 | convolution fusion | flops 81792000 | bytes 16916480 | tf_op jit(solution)/shard_map/while/body/eval_jaxpr/hqk,khd->qhd/dot_general | solution.py:87
  369.8 12.1 %fusion.145 = bf16[2,16,1024]{2,1,0:T(8,128)(2,1)S(1)} fusion(bf16[1024,2,16]{0,2,1:T(8,128)(2,1)S(1)} %bitcast.220, f32[2,1024,1024]{1,2,0:T(8,128)} %fusion.142, f32[2,1024,1024]{1,2,0:T(8,128)} %get-tuple-element.374, f32[2,1024]{1,0:T(2,128)S(1)} %get-tuple-element.375), kind=kOutput, calls=%fused_computation.35.clone.1 | convolution fusion | flops 81792000 | bytes 16916480 | tf_op jit(solution)/shard_map/while/body/eval_jaxpr/hqk,qhd->khd/dot_general | solution.py:90
  381.9 13.3 %fusion.144 = bf16[2,16,1024]{2,1,0:T(8,128)(2,1)S(1)} fusion(bf16[1024,2,16]{0,2,1:T(8,128)(2,1)S(1)} %bitcast.218, f32[2,1024,1024]{1,2,0:T(8,128)} %fusion.142, f32[2,1024,1024]{1,2,0:T(8,128)} %get-tuple-element.374, f32[2,1024]{1,0:T(2,128)S(1)} %get-tuple-element.375), kind=kOutput, calls=%fused_computation.36.clone.1 | convolution fusion | flops 81792000 | bytes 16916480 | tf_op jit(solution)/shard_map/while/body/eval_jaxpr/hqk,khd->qhd/dot_general | solution.py:87
  400.8 6.2 fusion.143
  411.5 12.1 %fusion.145 = bf16[2,16,1024]{2,1,0:T(8,128)(2,1)S(1)} fusion(bf16[1024,2,16]{0,2,1:T(8,128)(2,1)S(1)} %bitcast.220, f32[2,1024,1024]{1,2,0:T(8,128)} %fusion.142, f32[2,1024,1024]{1,2,0:T(8,128)} %get-tuple-element.374, f32[2,1024]{1,0:T(2,128)S(1)} %get-tuple-element.375), kind=kOutput, calls=%fused_computation.35.clone.1 | convolution fusion | flops 81792000 | bytes 16916480 | tf_op jit(solution)/shard_map/while/body/eval_jaxpr/hqk,qhd->khd/dot_general | solution.py:90
  423.6 13.3 %fusion.144 = bf16[2,16,1024]{2,1,0:T(8,128)(2,1)S(1)} fusion(bf16[1024,2,16]{0,2,1:T(8,128)(2,1)S(1)} %bitcast.218, f32[2,1024,1024]{1,2,0:T(8,128)} %fusion.142, f32[2,1024,1024]{1,2,0:T(8,128)} %get-tuple-element.374, f32[2,1024]{1,0:T(2,128)S(1)} %get-tuple-element.375), kind=kOutput, calls=%fused_computation.36.clone.1 | convolution fusion | flops 81792000 | bytes 16916480 | tf_op jit(solution)/shard_map/while/body/eval_jaxpr/hqk,khd->qhd/dot_general | solution.py:87
  442.6 6.2 fusion.143
  453.3 12.1 %fusion.145 = bf16[2,16,1024]{2,1,0:T(8,128)(2,1)S(1)} fusion(bf16[1024,2,16]{0,2,1:T(8,128)(2,1)S(1)} %bitcast.220, f32[2,1024,1024]{1,2,0:T(8,128)} %fusion.142, f32[2,1024,1024]{1,2,0:T(8,128)} %get-tuple-element.374, f32[2,1024]{1,0:T(2,128)S(1)} %get-tuple-element.375), kind=kOutput, calls=%fused_computation.35.clone.1 | convolution fusion | flops 81792000 | bytes 16916480 | tf_op jit(solution)/shard_map/while/body/eval_jaxpr/hqk,qhd->khd/dot_general | solution.py:90
  465.4 13.3 %fusion.144 = bf16[2,16,1024]{2,1,0:T(8,128)(2,1)S(1)} fusion(bf16[1024,2,16]{0,2,1:T(8,128)(2,1)S(1)} %bitcast.218, f32[2,1024,1024]{1,2,0:T(8,128)} %fusion.142, f32[2,1024,1024]{1,2,0:T(8,128)} %get-tuple-element.374, f32[2,1024]{1,0:T(2,128)S(1)} %get-tuple-element.375), kind=kOutput, calls=%fused_computation.36.clone.1 | convolution fusion | flops 81792000 | bytes 16916480 | tf_op jit(solution)/shard_map/while/body/eval_jaxpr/hqk,khd->qhd/dot_general | solution.py:87
  484.3 6.2 fusion.143
  495.0 12.1 %fusion.145 = bf16[2,16,1024]{2,1,0:T(8,128)(2,1)S(1)} fusion(bf16[1024,2,16]{0,2,1:T(8,128)(2,1)S(1)} %bitcast.220, f32[2,1024,1024]{1,2,0:T(8,128)} %fusion.142, f32[2,1024,1024]{1,2,0:T(8,128)} %get-tuple-element.374, f32[2,1024]{1,0:T(2,128)S(1)} %get-tuple-element.375), kind=kOutput, calls=%fused_computation.35.clone.1 | convolution fusion | flops 81792000 | bytes 16916480 | tf_op jit(solution)/shard_map/while/body/eval_jaxpr/hqk,qhd->khd/dot_general | solution.py:90
  507.1 13.3 %fusion.144 = bf16[2,16,1024]{2,1,0:T(8,128)(2,1)S(1)} fusion(bf16[1024,2,16]{0,2,1:T(8,128)(2,1)S(1)} %bitcast.218, f32[2,1024,1024]{1,2,0:T(8,128)} %fusion.142, f32[2,1024,1024]{1,2,0:T(8,128)} %get-tuple-element.374, f32[2,1024]{1,0:T(2,128)S(1)} %get-tuple-element.375), kind=kOutput, calls=%fused_computation.36.clone.1 | convolution fusion | flops 81792000 | bytes 16916480 | tf_op jit(solution)/shard_map/while/body/eval_jaxpr/hqk,khd->qhd/dot_general | solution.py:87
  526.1 6.2 fusion.143
  536.7 12.1 %fusion.145 = bf16[2,16,1024]{2,1,0:T(8,128)(2,1)S(1)} fusion(bf16[1024,2,16]{0,2,1:T(8,128)(2,1)S(1)} %bitcast.220, f32[2,1024,1024]{1,2,0:T(8,128)} %fusion.142, f32[2,1024,1024]{1,2,0:T(8,128)} %get-tuple-element.374, f32[2,1024]{1,0:T(2,128)S(1)} %get-tuple-element.375), kind=kOutput, calls=%fused_computation.35.clone.1 | convolution fusion | flops 81792000 | bytes 16916480 | tf_op jit(solution)/shard_map/while/body/eval_jaxpr/hqk,qhd->khd/dot_general | solution.py:90
  548.8 13.3 %fusion.144 = bf16[2,16,1024]{2,1,0:T(8,128)(2,1)S(1)} fusion(bf16[1024,2,16]{0,2,1:T(8,128)(2,1)S(1)} %bitcast.218, f32[2,1024,1024]{1,2,0:T(8,128)} %fusion.142, f32[2,1024,1024]{1,2,0:T(8,128)} %get-tuple-element.374, f32[2,1024]{1,0:T(2,128)S(1)} %get-tuple-element.375), kind=kOutput, calls=%fused_computation.36.clone.1 | convolution fusion | flops 81792000 | bytes 16916480 | tf_op jit(solution)/shard_map/while/body/eval_jaxpr/hqk,khd->qhd/dot_general | solution.py:87
  567.8 6.2 fusion.143
  578.5 12.1 %fusion.145 = bf16[2,16,1024]{2,1,0:T(8,128)(2,1)S(1)} fusion(bf16[1024,2,16]{0,2,1:T(8,128)(2,1)S(1)} %bitcast.220, f32[2,1024,1024]{1,2,0:T(8,128)} %fusion.142, f32[2,1024,1024]{1,2,0:T(8,128)} %get-tuple-element.374, f32[2,1024]{1,0:T(2,128)S(1)} %get-tuple-element.375), kind=kOutput, calls=%fused_computation.35.clone.1 | convolution fusion | flops 81792000 | bytes 16916480 | tf_op jit(solution)/shard_map/while/body/eval_jaxpr/hqk,qhd->khd/dot_general | solution.py:90
  590.6 13.3 %fusion.144 = bf16[2,16,1024]{2,1,0:T(8,128)(2,1)S(1)} fusion(bf16[1024,2,16]{0,2,1:T(8,128)(2,1)S(1)} %bitcast.218, f32[2,1024,1024]{1,2,0:T(8,128)} %fusion.142, f32[2,1024,1024]{1,2,0:T(8,128)} %get-tuple-element.374, f32[2,1024]{1,0:T(2,128)S(1)} %get-tuple-element.375), kind=kOutput, calls=%fused_computation.36.clone.1 | convolution fusion | flops 81792000 | bytes 16916480 | tf_op jit(solution)/shard_map/while/body/eval_jaxpr/hqk,khd->qhd/dot_general | solution.py:87
  620.2 12.1 %fusion.145 = bf16[2,16,1024]{2,1,0:T(8,128)(2,1)S(1)} fusion(bf16[1024,2,16]{0,2,1:T(8,128)(2,1)S(1)} %bitcast.220, f32[2,1024,1024]{1,2,0:T(8,128)} %fusion.142, f32[2,1024,1024]{1,2,0:T(8,128)} %get-tuple-element.374, f32[2,1024]{1,0:T(2,128)S(1)} %get-tuple-element.375), kind=kOutput, calls=%fused_computation.35.clone.1 | convolution fusion | flops 81792000 | bytes 16916480 | tf_op jit(solution)/shard_map/while/body/eval_jaxpr/hqk,qhd->khd/dot_general | solution.py:90
  632.3 13.3 %fusion.144 = bf16[2,16,1024]{2,1,0:T(8,128)(2,1)S(1)} fusion(bf16[1024,2,16]{0,2,1:T(8,128)(2,1)S(1)} %bitcast.218, f32[2,1024,1024]{1,2,0:T(8,128)} %fusion.142, f32[2,1024,1024]{1,2,0:T(8,128)} %get-tuple-element.374, f32[2,1024]{1,0:T(2,128)S(1)} %get-tuple-element.375), kind=kOutput, calls=%fused_computation.36.clone.1 | convolution fusion | flops 81792000 | bytes 16916480 | tf_op jit(solution)/shard_map/while/body/eval_jaxpr/hqk,khd->qhd/dot_general | solution.py:87
  662.0 12.1 %fusion.145 = bf16[2,16,1024]{2,1,0:T(8,128)(2,1)S(1)} fusion(bf16[1024,2,16]{0,2,1:T(8,128)(2,1)S(1)} %bitcast.220, f32[2,1024,1024]{1,2,0:T(8,128)} %fusion.142, f32[2,1024,1024]{1,2,0:T(8,128)} %get-tuple-element.374, f32[2,1024]{1,0:T(2,128)S(1)} %get-tuple-element.375), kind=kOutput, calls=%fused_computation.35.clone.1 | convolution fusion | flops 81792000 | bytes 16916480 | tf_op jit(solution)/shard_map/while/body/eval_jaxpr/hqk,qhd->khd/dot_general | solution.py:90
  674.1 13.3 %fusion.144 = bf16[2,16,1024]{2,1,0:T(8,128)(2,1)S(1)} fusion(bf16[1024,2,16]{0,2,1:T(8,128)(2,1)S(1)} %bitcast.218, f32[2,1024,1024]{1,2,0:T(8,128)} %fusion.142, f32[2,1024,1024]{1,2,0:T(8,128)} %get-tuple-element.374, f32[2,1024]{1,0:T(2,128)S(1)} %get-tuple-element.375), kind=kOutput, calls=%fused_computation.36.clone.1 | convolution fusion | flops 81792000 | bytes 16916480 | tf_op jit(solution)/shard_map/while/body/eval_jaxpr/hqk,khd->qhd/dot_general | solution.py:87
  703.7 12.1 %fusion.145 = bf16[2,16,1024]{2,1,0:T(8,128)(2,1)S(1)} fusion(bf16[1024,2,16]{0,2,1:T(8,128)(2,1)S(1)} %bitcast.220, f32[2,1024,1024]{1,2,0:T(8,128)} %fusion.142, f32[2,1024,1024]{1,2,0:T(8,128)} %get-tuple-element.374, f32[2,1024]{1,0:T(2,128)S(1)} %get-tuple-element.375), kind=kOutput, calls=%fused_computation.35.clone.1 | convolution fusion | flops 81792000 | bytes 16916480 | tf_op jit(solution)/shard_map/while/body/eval_jaxpr/hqk,qhd->khd/dot_general | solution.py:90
  715.8 13.3 %fusion.144 = bf16[2,16,1024]{2,1,0:T(8,128)(2,1)S(1)} fusion(bf16[1024,2,16]{0,2,1:T(8,128)(2,1)S(1)} %bitcast.218, f32[2,1024,1024]{1,2,0:T(8,128)} %fusion.142, f32[2,1024,1024]{1,2,0:T(8,128)} %get-tuple-element.374, f32[2,1024]{1,0:T(2,128)S(1)} %get-tuple-element.375), kind=kOutput, calls=%fused_computation.36.clone.1 | convolution fusion | flops 81792000 | bytes 16916480 | tf_op jit(solution)/shard_map/while/body/eval_jaxpr/hqk,khd->qhd/dot_general | solution.py:87
  745.5 12.1 %fusion.145 = bf16[2,16,1024]{2,1,0:T(8,128)(2,1)S(1)} fusion(bf16[1024,2,16]{0,2,1:T(8,128)(2,1)S(1)} %bitcast.220, f32[2,1024,1024]{1,2,0:T(8,128)} %fusion.142, f32[2,1024,1024]{1,2,0:T(8,128)} %get-tuple-element.374, f32[2,1024]{1,0:T(2,128)S(1)} %get-tuple-element.375), kind=kOutput, calls=%fused_computation.35.clone.1 | convolution fusion | flops 81792000 | bytes 16916480 | tf_op jit(solution)/shard_map/while/body/eval_jaxpr/hqk,qhd->khd/dot_general | solution.py:90
  757.6 13.3 %fusion.144 = bf16[2,16,1024]{2,1,0:T(8,128)(2,1)S(1)} fusion(bf16[1024,2,16]{0,2,1:T(8,128)(2,1)S(1)} %bitcast.218, f32[2,1024,1024]{1,2,0:T(8,128)} %fusion.142, f32[2,1024,1024]{1,2,0:T(8,128)} %get-tuple-element.374, f32[2,1024]{1,0:T(2,128)S(1)} %get-tuple-element.375), kind=kOutput, calls=%fused_computation.36.clone.1 | convolution fusion | flops 81792000 | bytes 16916480 | tf_op jit(solution)/shard_map/while/body/eval_jaxpr/hqk,khd->qhd/dot_general | solution.py:87
  791.4 188.2 %while.30 = (s32[]{:T(128)}, bf16[1024,512]{0,1:T(8,128)(2,1)}, bf16[1024,1536]{0,1:T(8,128)(2,1)}, pred[1024]{0:T(1024)(128)(4,1)S(1)}, s32[]{:T(128)}, /*index...) while((s32[]{:T(128)}, bf16[1024,512]{0,1:T(8,128)(2,1)}, ...), condition=%wide.region_8.10_spmd, body=%wide.region_5.9_spmd.sunk | while | flops 146801680 | bytes 17581340 | solution.py:59
  792.3 6.2 fusion.130
  804.1 6.2 fusion.130
  815.8 6.2 fusion.130
  839.4 6.2 fusion.130
  851.1 6.2 fusion.130
  862.9 6.2 fusion.130
  874.6 6.2 fusion.130
  886.4 6.2 fusion.130
  898.2 6.2 fusion.130
  909.9 6.2 fusion.130
  921.7 6.2 fusion.130
  933.5 6.2 fusion.130
  945.2 6.2 fusion.130
  957.0 6.2 fusion.130
  968.8 6.2 fusion.130
  994.1 15.2 %collective-permute-done.6 = bf16[1,128,1536]{2,1,0:T(8,128)(2,1)S(1)} collective-permute-done((bf16[1,128,1536]{2,1,0:T(8,128)(2,1)}, bf16[1,128,1536]{2,1,0:T(8,128)(2,1)S(1)}, u32[]{:S(2)}, u32[]{:S(2)}) %collective-permute-start.6) | collective-permute-done | bytes 393248 | tf_op jit(solution)/shard_map/ppermute | solution.py:184
  1009.3 7.4 collective-permute-done.7
  1042.9 6.5 collective-permute-done
  (310 shorter events, 423.3 us)
Async XLA Ops:
  0.6 7.2 copy-start
  0.6 7.8 copy-start.16
  0.7 8.9 copy-start.8
  0.7 9.4 copy-start.27
  3.0 26.9 %all-to-all-start.4 = ((bf16[8,1,128]{2,1,0:T(2,128)(2,1)}), bf16[8,1,128]{2,1,0:T(2,128)(2,1)S(1)}, u32[]{:S(2)}, u32[]{:S(2)}) async-start(bf16[8,1,128]{2,1,0:T(2,128)(2,1)} %compare_convert_fusion), calls=%async_computation.4 | async-start | bytes 8192 | tf_op jit(solution)/shard_map/all_to_all | solution.py:159
  8.1 1.9 copy-start.2
  8.2 1.8 copy-start.14
  8.4 1.6 copy-start.19
  8.4 1.6 copy-start.17
  10.0 2.7 copy-start.9
  10.1 2.7 copy-start.26
  19.4 4.0 copy-start.6
  19.4 4.0 copy-start.11
  29.9 7.3 all-to-all-start.1
  37.2 18.8 %all-to-all-start.5 = ((bf16[8,128,512]{2,1,0:T(8,128)(2,1)}), bf16[8,128,512]{2,1,0:T(8,128)(2,1)S(1)}, u32[]{:S(2)}, u32[]{:S(2)}) async-start(bf16[8,128,512]{2,1,0:T(8,128)(2,1)} %select_select_fusion), calls=%async_computation.5 | async-start | bytes 2097152 | tf_op jit(solution)/shard_map/all_to_all | solution.py:161
  56.0 1.0 copy-start.5
  57.0 41.5 %all-to-all-start.3 = ((bf16[8,128,1536]{2,1,0:T(8,128)(2,1)}), bf16[8,128,1536]{2,1,0:T(8,128)(2,1)S(1)}, u32[]{:S(2)}, u32[]{:S(2)}) async-start(bf16[8,128,1536]{2,1,0:T(8,128)(2,1)} %broadcast_select_fusion.2), calls=%async_computation.3 | async-start | bytes 6291456 | tf_op jit(solution)/shard_map/all_to_all | solution.py:158
  98.5 687.1 %all-to-all-start = ((bf16[8,128,1536]{2,1,0:T(8,128)(2,1)}), bf16[8,128,1536]{2,1,0:T(8,128)(2,1)}, u32[]{:S(2)}, u32[]{:S(2)}) async-start(bf16[8,128,1536]{2,1,0:T(8,128)(2,1)} %broadcast_select_fusion.3), calls=%async_computation | async-start | bytes 6291456 | tf_op jit(solution)/shard_map/all_to_all | solution.py:154
  778.5 1.9 copy-start.4
  781.9 204.5 %collective-permute-start.1 = (bf16[1,128,1536]{2,1,0:T(8,128)(2,1)}, bf16[1,128,1536]{2,1,0:T(8,128)(2,1)}, u32[]{:S(2)}, u32[]{:S(2)}) collective-permute-start(bf16[1,128,1536]{2,1,0:T(8,128)(2,1)} %get-tuple-element.292), channel_id=1, source_target_pairs={{0,1},{1,0},{2,3},{3,2},{4,5},{5,4},{6,7},{7,6},{8,9},{9,8},{10,11... | collective-permute-start | bytes 1179656 | tf_op jit(solution)/shard_map/ppermute | solution.py:184
  782.1 206.9 %collective-permute-start.2 = (bf16[1,128,1536]{2,1,0:T(8,128)(2,1)}, bf16[1,128,1536]{2,1,0:T(8,128)(2,1)}, u32[]{:S(2)}, u32[]{:S(2)}) collective-permute-start(bf16[1,128,1536]{2,1,0:T(8,128)(2,1)} %get-tuple-element.291), channel_id=1, source_target_pairs={{0,2},{1,3},{2,0},{3,1},{4,6},{5,7},{6,4},{7,5},{8,10},{9,11},{10,... | collective-permute-start | bytes 1179656 | tf_op jit(solution)/shard_map/ppermute | solution.py:184
  782.4 208.6 %collective-permute-start.3 = (bf16[1,128,1536]{2,1,0:T(8,128)(2,1)}, bf16[1,128,1536]{2,1,0:T(8,128)(2,1)}, u32[]{:S(2)}, u32[]{:S(2)}) collective-permute-start(bf16[1,128,1536]{2,1,0:T(8,128)(2,1)} %get-tuple-element.290), channel_id=1, source_target_pairs={{0,3},{1,2},{2,1},{3,0},{4,7},{5,6},{6,5},{7,4},{8,11},{9,10},{10,... | collective-permute-start | bytes 1179656 | tf_op jit(solution)/shard_map/ppermute | solution.py:184
  783.8 208.3 %collective-permute-start.4 = (bf16[1,128,1536]{2,1,0:T(8,128)(2,1)}, bf16[1,128,1536]{2,1,0:T(8,128)(2,1)}, u32[]{:S(2)}, u32[]{:S(2)}) collective-permute-start(bf16[1,128,1536]{2,1,0:T(8,128)(2,1)} %get-tuple-element.289), channel_id=1, source_target_pairs={{0,4},{1,5},{2,6},{3,7},{4,0},{5,1},{6,2},{7,3},{8,12},{9,13},{10,... | collective-permute-start | bytes 1179656 | tf_op jit(solution)/shard_map/ppermute | solution.py:184
  785.3 207.8 %collective-permute-start.5 = (bf16[1,128,1536]{2,1,0:T(8,128)(2,1)}, bf16[1,128,1536]{2,1,0:T(8,128)(2,1)}, u32[]{:S(2)}, u32[]{:S(2)}) collective-permute-start(bf16[1,128,1536]{2,1,0:T(8,128)(2,1)} %get-tuple-element.288), channel_id=1, source_target_pairs={{0,5},{1,4},{2,7},{3,6},{4,1},{5,0},{6,3},{7,2},{8,13},{9,12},{10,... | collective-permute-start | bytes 1179656 | tf_op jit(solution)/shard_map/ppermute | solution.py:184
  785.6 5.8 copy-start.23
  979.6 9.4 copy-start.13
  981.9 45.0 %all-to-all-start.2 = ((bf16[8,128,512]{2,1,0:T(8,128)(2,1)}), bf16[8,128,512]{2,1,0:T(8,128)(2,1)}, u32[]{:S(2)}, u32[]{:S(2)}) async-start(bf16[8,128,512]{2,1,0:T(8,128)(2,1)} %bitcast.209), calls=%async_computation.2 | async-start | bytes 2097152 | tf_op jit(solution)/shard_map/all_to_all | solution.py:171
  986.4 30.4 %copy-start.22 = (s32[1024]{0:T(1024)S(1)}, s32[1024]{0:T(1024)}, u32[]{:S(2)}) copy-start(s32[1024]{0:T(1024)} %pad_clamp_fusion) | copy-start | bytes 12292
  986.4 22.9 %collective-permute-start.6 = (bf16[1,128,1536]{2,1,0:T(8,128)(2,1)}, bf16[1,128,1536]{2,1,0:T(8,128)(2,1)S(1)}, u32[]{:S(2)}, u32[]{:S(2)}) collective-permute-start(bf16[1,128,1536]{2,1,0:T(8,128)(2,1)} %get-tuple-element.287), channel_id=1, source_target_pairs={{0,6},{1,7},{2,4},{3,5},{4,2},{5,3},{6,0},{7,1},{8,14},{9,15},{10,... | collective-permute-start | bytes 1179656 | tf_op jit(solution)/shard_map/ppermute | solution.py:184
  989.0 27.8 %collective-permute-start.7 = (bf16[1,128,1536]{2,1,0:T(8,128)(2,1)S(1)}, bf16[1,128,1536]{2,1,0:T(8,128)(2,1)S(1)}, u32[]{:S(2)}, u32[]{:S(2)}) collective-permute-start(bf16[1,128,1536]{2,1,0:T(8,128)(2,1)S(1)} %copy-done.13), channel_id=1, source_target_pairs={{0,7},{1,6},{2,5},{3,4},{4,3},{5,2},{6,1},{7,0},{8,15},{9,14},{10,... | collective-permute-start | bytes 1179656 | tf_op jit(solution)/shard_map/ppermute | solution.py:184
  1016.8 3.0 copy-start.15
  1016.8 3.0 copy-start.25
  1016.8 3.0 copy-start.28
  1019.8 3.2 copy-start.20
  1019.8 3.2 copy-start.3
  1019.8 3.2 copy-start.18
  1019.8 3.5 copy-start.7
  1023.0 3.9 copy-start.21
  1023.4 7.7 copy-start.10
  1023.4 7.7 copy-start.12
  1023.4 7.7 copy-start.24
  1024.5 16.3 %collective-permute-start.8 = (bf16[1,512,512]{1,2,0:T(8,128)(2,1)}, bf16[1,512,512]{1,2,0:T(8,128)(2,1)}, u32[]{:S(2)}, u32[]{:S(2)}) collective-permute-start(bf16[1,512,512]{1,2,0:T(8,128)(2,1)} %fusion.64), channel_id=1, source_target_pairs={{8,0},{16,8},{24,16},{9,1},{17,9},{25,17},{10,2},{18,10},{26,18},{... | collective-permute-start | bytes 1572872 | tf_op jit(solution)/shard_map/ppermute | solution.py:17
  1026.9 23.3 %copy-start.1 = (bf16[1,4,512,512]{3,2,1,0:T(8,128)(2,1)S(1)}, bf16[1,4,512,512]{3,2,1,0:T(8,128)(2,1)}, u32[]{:S(2)}) copy-start(bf16[1,4,512,512]{3,2,1,0:T(8,128)(2,1)} %param.16) | copy-start | bytes 6291460
  1033.4 15.9 %collective-permute-start = (bf16[1,512,512]{2,1,0:T(8,128)(2,1)}, bf16[1,512,512]{2,1,0:T(8,128)(2,1)S(1)}, u32[]{:S(2)}, u32[]{:S(2)}) collective-permute-start(bf16[1,512,512]{2,1,0:T(8,128)(2,1)} %fusion.48), channel_id=1, source_target_pairs={{0,8},{8,16},{16,24},{1,9},{9,17},{17,25},{2,10},{10,18},{18,26},{... | collective-permute-start | bytes 1572872 | tf_op jit(solution)/shard_map/ppermute | solution.py:17
